TPU v7x, 32 devices: a whole 2x2x4 slice. The times are simulated.
32 devices in a mesh: dp: 8 (over z, x), mp: 4 (over y, core).
Axes of the slice: x: 2, y: 2, z: 4, core: 2. Of those that a mesh axis runs over, the one named last changes fastest.
Arguments:
- tokens: bfloat16 [2048, 8192], P('dp', 'mp'), may hold values from -6 to 6
- cotangent: bfloat16 [2048, 8192], P('dp', 'mp'), may hold values from -6 to 6
- w_in: bfloat16 [64, 4, 256, 256], P('mp'), may hold values from -0.1875 to 0.1875
- w_out: bfloat16 [64, 4, 256, 256], P('mp'), may hold values from -0.125 to 0.125
- in_blocks: int32 [64, 4], P('mp'), may hold values from 0 to 31, as said below
- out_blocks: int32 [64, 4], P('mp'), may hold values from 0 to 31, as said below
Outputs:
- output: bfloat16 [2048, 8192], P('dp', 'mp')
- grad_tokens: bfloat16 [2048, 8192], P('dp', 'mp')
- grad_in: float32 [64, 4, 256, 256], P('mp', None, 'dp')
- grad_out: float32 [64, 4, 256, 256], P('mp', None, 'dp')
Inputs may be any that keep to these rules, and one draw needn't show every extreme that they name: `in_blocks`: flat butterfly pattern: row j holds p(j mod 32 XOR m) for m = 0, 1, 2, 4, with p a permutation of the 32 input blocks; the 4 entries of a row differ and every block is named by exactly 8 rows. `out_blocks`: the same flat butterfly form with its own permutation q of the 32 output blocks.
All inputs are finite; a program needn't handle non-finite values.
Results may differ from a plain program's by a relative error of at most 0.018.
Values may be sent and summed in bfloat16 or wider, within the bound.
A program may use at most 128 MiB of HBM per device.

v0:
```python
import math

import jax
import jax.numpy as jnp
from jax import lax
from jax.sharding import PartitionSpec as P

MB = 2


def place_blocks(values, targets, row_blocks):
    step_tok = values.shape[0]
    side = values.shape[-1]
    flat = values.reshape(step_tok, -1, side)
    placed = (
        jnp.zeros((step_tok, row_blocks, side), jnp.float32).at[:, targets.reshape(-1)].add(flat)
    )
    return placed.reshape(step_tok, row_blocks * side)


def shards(tokens, cotangent, w_in, w_out, in_blocks, out_blocks):
    hb_dev, kk, side, _ = w_in.shape
    total_tok = tokens.shape[0]
    width = tokens.shape[1] * lax.axis_size("mp")
    row_blocks = width // side
    passes = MB
    step_tok = total_tok // passes
    grad_in = jnp.zeros(w_in.shape, jnp.float32)
    grad_out = jnp.zeros(w_out.shape, jnp.float32)
    out_share = None
    outputs = []
    backs = []
    for index in range(passes):
        x_part = tokens[index * step_tok : (index + 1) * step_tok]
        dy_part = cotangent[index * step_tok : (index + 1) * step_tok]
        x_full = lax.all_gather(x_part, "mp", axis=1, tiled=True)
        selected = x_full.reshape(step_tok, row_blocks, side)[:, in_blocks]
        pre = jnp.einsum("tjkb,jkbc->tjc", selected, w_in, preferred_element_type=jnp.float32)
        act = jax.nn.gelu(pre).astype(jnp.bfloat16)
        terms = jnp.einsum("tjb,jkbc->tjkc", act, w_out, preferred_element_type=jnp.float32)
        partial_out = place_blocks(terms, out_blocks, row_blocks)
        outputs.append(
            lax.psum_scatter(
                partial_out.astype(jnp.bfloat16), "mp", scatter_dimension=1, tiled=True
            )
        )
        dy_full = lax.all_gather(dy_part, "mp", axis=1, tiled=True)
        picked = dy_full.reshape(step_tok, row_blocks, side)[:, out_blocks]
        d_act = jnp.einsum("tjkc,jkbc->tjb", picked, w_out, preferred_element_type=jnp.float32)
        _, pullback = jax.vjp(jax.nn.gelu, pre)
        d_pre = pullback(d_act)[0].astype(jnp.bfloat16)
        grad_out = grad_out + jnp.einsum(
            "tjb,tjkc->jkbc", act, picked, preferred_element_type=jnp.float32
        )
        grad_in = grad_in + jnp.einsum(
            "tjkb,tjc->jkbc", selected, d_pre, preferred_element_type=jnp.float32
        )
        back = jnp.einsum("tjc,jkbc->tjkb", d_pre, w_in, preferred_element_type=jnp.float32)
        partial_back = place_blocks(back, in_blocks, row_blocks)
        backs.append(
            lax.psum_scatter(
                partial_back.astype(jnp.bfloat16), "mp", scatter_dimension=1, tiled=True
            )
        )
    scale = 1.0 / math.sqrt(total_tok * lax.axis_size("dp"))
    in_share, out_share = (
        lax.psum_scatter(
            grad_in.astype(jnp.bfloat16), "dp", scatter_dimension=2, tiled=True
        ).astype(jnp.float32),
        lax.psum_scatter(
            grad_out.astype(jnp.bfloat16), "dp", scatter_dimension=2, tiled=True
        ).astype(jnp.float32),
    )
    output = jnp.concatenate(outputs, axis=0)
    grad_tokens = jnp.concatenate(backs, axis=0)
    return (output, grad_tokens, in_share * scale, out_share * scale)


def solution(mesh):
    placed = (
        P("dp", "mp"),
        P("dp", "mp"),
        P("mp", None, None, None),
        P("mp", None, None, None),
        P("mp", None),
        P("mp", None),
    )
    return jax.shard_map(
        shards,
        mesh=mesh,
        in_specs=placed,
        out_specs=(
            P("dp", "mp"),
            P("dp", "mp"),
            P("mp", None, "dp", None),
            P("mp", None, "dp", None),
        ),
        check_vma=False,
    )
```

profile of v0, /device:TPU:0, one launch (start us, length us, event | category | flops | bytes accessed | tf_op | source)
XLA Modules:
  0.0 609.1 jit_solution(17895113420931829797)
XLA Ops:
  13.6 21.8 %all-gather.5.cloned.1.call-done = bf16[128,8192]{0,1:T(8,128)(2,1)} async-done(((bf16[128,2048]{0,1:T(8,128)(2,1)}), bf16[128,8192]{0,1:T(8,128)(2,1)}) %all-gather.5.cloned.1.call-update) | async-done | bytes 2097168 | tf_op jit(solution)/shard_map/all_gather | solution.py:36
  35.4 3.3 copy.47
  38.7 21.5 %all-gather.9.cloned.1.call-done = bf16[128,8192]{0,1:T(8,128)(2,1)} async-done(((bf16[128,2048]{0,1:T(8,128)(2,1)}), bf16[128,8192]{0,1:T(8,128)(2,1)}) %all-gather.9.cloned.1.call-update) | async-done | bytes 2097168 | tf_op jit(solution)/shard_map/all_gather | solution.py:47
  60.2 4.1 copy.59
  64.2 2.8 gather_fusion
  67.0 4.5 gather_fusion.2
  71.5 6.1 fusion.45
  77.6 6.8 %fusion.30 = bf16[128,16,256,1]{2,0,3,1:T(8,128)(2,1)S(1)} fusion(f32[16,128,256,1]{2,1,3,0:T(8,128)S(1)} %fusion.45, bf16[128,16,4,256]{3,0,2,1:T(8,128)(2,1)S(1)} %bitcast.193, bf16[16,4,256,256]{3,2,1,0:T(8,128)(2,1)} %param.9), kind=kOutput, calls=%fused_computation.52 | convolution fusion | flops 1084227584 | bytes 15728640 | tf_op jit(solution)/shard_map/tjkc,jkbc->tjb/dot_general | solution.py:49
  84.4 6.1 fusion.47
  90.5 2.4 broadcast.63.clone.3
  92.9 19.1 %scatter_fusion.2 = f32[128,32,256]{2,0,1:T(8,128)} fusion(f32[128,32,256]{2,0,1:T(8,128)} %broadcast.63.clone.3, s32[64]{0:T(128)S(1)} %fusion.38, f32[64,128,256]{2,1,0:T(8,128)} %bitcast.191), kind=kCustom, calls=%fused_computation.6 | custom fusion | flops 2097152 | bytes 25166080 | tf_op jit(solution)/shard_map/scatter-add | solution.py:16
  112.0 3.8 convert_element_type.58
  115.8 4.1 copy.62
  120.2 4.1 copy.52
  124.2 4.7 gather_fusion.1
  128.9 4.1 copy.64
  133.0 4.3 gather_fusion.3
  137.3 6.0 fusion.46
  143.4 8.7 %fusion.29 = bf16[128,16,256,1]{2,0,3,1:T(8,128)(2,1)S(1)} fusion(f32[16,128,256,1]{2,1,3,0:T(8,128)S(1)} %fusion.46, bf16[128,16,4,256]{3,0,2,1:T(8,128)(2,1)} %bitcast.194, bf16[16,4,256,256]{3,2,1,0:T(8,128)(2,1)} %param.9), kind=kOutput, calls=%fused_computation.51 | convolution fusion | flops 1084227584 | bytes 15728640 | tf_op jit(solution)/shard_map/tjkc,jkbc->tjb/dot_general | solution.py:49
  152.1 6.1 fusion.48
  158.2 2.5 broadcast.63.clone.2
  160.7 18.6 %scatter_fusion.3 = f32[128,32,256]{2,0,1:T(8,128)} fusion(f32[128,32,256]{2,0,1:T(8,128)} %broadcast.63.clone.2, s32[64]{0:T(128)S(1)} %fusion.38, f32[64,128,256]{2,1,0:T(8,128)} %bitcast.190), kind=kCustom, calls=%fused_computation.7 | custom fusion | flops 2097152 | bytes 25166080 | tf_op jit(solution)/shard_map/scatter-add | solution.py:16
  179.2 3.8 convert_element_type.61
  183.0 4.1 copy.67
  187.6 8.4 %fusion.35 = f32[16,128,4,256]{3,1,2,0:T(8,128)} fusion(bf16[16,4,256,256]{3,2,1,0:T(8,128)(2,1)} %param.9, f32[16,128,256,1]{2,1,3,0:T(8,128)S(1)} %fusion.45), kind=kOutput, calls=%fused_computation.59 | convolution fusion | flops 1078460416 | bytes 18874368 | tf_op jit(solution)/shard_map/tjb,jkbc->tjkc/dot_general | solution.py:40
  196.0 2.4 broadcast.63.clone.1
  198.5 18.7 %scatter_fusion = f32[128,32,256]{2,0,1:T(8,128)} fusion(f32[128,32,256]{2,0,1:T(8,128)} %broadcast.63.clone.1, s32[64]{0:T(128)S(1)} %fusion.37, f32[64,128,256]{2,1,0:T(8,128)} %bitcast.185), kind=kCustom, calls=%fused_computation.4 | custom fusion | flops 2097152 | bytes 25166080 | tf_op jit(solution)/shard_map/scatter-add | solution.py:16
  217.1 3.8 convert_element_type.52
  221.0 4.1 copy.50
  225.1 9.1 %fusion.32 = f32[16,128,4,256]{3,1,2,0:T(8,128)} fusion(bf16[16,4,256,256]{3,2,1,0:T(8,128)(2,1)} %param.9, f32[16,128,256,1]{2,1,3,0:T(8,128)} %copy-done), kind=kOutput, calls=%fused_computation.56 | convolution fusion | flops 1078460416 | bytes 18874368 | tf_op jit(solution)/shard_map/tjb,jkbc->tjkc/dot_general | solution.py:40
  234.2 2.4 broadcast.63.clone
  236.7 18.8 %scatter_fusion.1 = f32[128,32,256]{2,0,1:T(8,128)} fusion(f32[128,32,256]{2,0,1:T(8,128)} %broadcast.63.clone, s32[64]{0:T(128)S(1)} %fusion.37, f32[64,128,256]{2,1,0:T(8,128)} %bitcast.184), kind=kCustom, calls=%fused_computation.5 | custom fusion | flops 2097152 | bytes 25166080 | tf_op jit(solution)/shard_map/scatter-add | solution.py:16
  255.4 3.8 convert_element_type.55
  259.3 4.1 copy.55
  263.4 6.4 %copy.48 = bf16[16,4,128,256]{2,3,1,0:T(8,128)(2,1)} copy(bf16[16,4,128,256]{3,2,1,0:T(8,128)(2,1)} %bitcast.187) | data formatting | bytes 8388608 | tf_op jit(solution)/shard_map/gather | solution.py:37
  269.9 6.5 %copy.53 = bf16[16,4,128,256]{2,3,1,0:T(8,128)(2,1)} copy(bf16[16,4,128,256]{3,2,1,0:T(8,128)(2,1)} %bitcast.189) | data formatting | bytes 8388608 | tf_op jit(solution)/shard_map/gather | solution.py:37
  276.4 10.3 %fusion.5 = f32[16,4,256,256]{3,2,1,0:T(8,128)} fusion(bf16[128,16,256,1]{2,0,3,1:T(8,128)(2,1)S(1)} %fusion.30, bf16[16,4,128,256]{2,3,1,0:T(8,128)(2,1)} %copy.48), kind=kOutput, calls=%fused_computation.15 | convolution fusion | flops 1073741824 | bytes 22020096 | tf_op jit(solution)/shard_map/tjkb,tjc->jkbc/dot_general | solution.py:55
  286.6 13.0 %add_convert_fusion.1 = bf16[16,4,256,256]{3,2,1,0:T(8,128)(2,1)} fusion(f32[16,4,256,256]{3,2,1,0:T(8,128)} %fusion.5, bf16[128,16,256,1]{2,0,3,1:T(8,128)(2,1)} %copy-done.2, bf16[16,4,128,256]{2,3,1,0:T(8,128)(2,1)} %copy.53), kind=kOutput, calls=%fused_computation.9 | convolution fusion | flops 1082130432 | bytes 30408704 | tf_op jit(solution)/shard_map/tjkb,tjc->jkbc/dot_general | solution.py:55
  300.0 6.4 %copy.60 = bf16[16,4,128,256]{2,3,1,0:T(8,128)(2,1)} copy(bf16[16,4,128,256]{3,2,1,0:T(8,128)(2,1)} %bitcast.192) | data formatting | bytes 8388608 | tf_op jit(solution)/shard_map/gather | solution.py:48
  306.4 6.4 %copy.65 = bf16[16,4,128,256]{2,3,1,0:T(8,128)(2,1)} copy(bf16[16,4,128,256]{3,2,1,0:T(8,128)(2,1)} %bitcast.195) | data formatting | bytes 8388608 | tf_op jit(solution)/shard_map/gather | solution.py:48
  312.9 10.3 %fusion.2 = f32[16,4,256,256]{2,3,1,0:T(8,128)} fusion(bf16[16,4,128,256]{2,3,1,0:T(8,128)(2,1)} %copy.60, f32[16,128,256,1]{2,1,3,0:T(8,128)S(1)} %fusion.45), kind=kOutput, calls=%fused_computation.12 | convolution fusion | flops 1078460416 | bytes 23068672 | tf_op jit(solution)/shard_map/tjb,tjkc->jkbc/dot_general | solution.py:52
  323.2 13.5 %fusion = bf16[16,4,256,256]{3,2,1,0:T(8,128)(2,1)} fusion(f32[16,4,256,256]{2,3,1,0:T(8,128)} %fusion.2, bf16[16,4,128,256]{2,3,1,0:T(8,128)(2,1)} %copy.65, f32[16,128,256,1]{2,1,3,0:T(8,128)} %copy-done), kind=kOutput, calls=%fused_computation.10 | convolution fusion | flops 1086849024 | bytes 31457280 | tf_op jit(solution)/shard_map/tjb,tjkc->jkbc/dot_general | solution.py:52
  338.1 1.4 copy.71
  340.8 1.4 copy.70
  342.3 106.3 %reduce-scatter.15.cloned.1.call-done = bf16[16,4,32,256]{3,2,1,0:T(8,128)(2,1)} async-done(((bf16[16,4,256,256]{3,2,1,0:T(8,128)(2,1)}), bf16[16,4,32,256]{3,2,1,0:T(8,128)(2,1)}) %reduce-scatter.15.cloned.1.call-update) | async-done | bytes 1048592 | tf_op jit(solution)/shard_map/reduce_scatter | solution.py:67
  448.6 2.8 convert_multiply_fusion.1
  451.4 147.6 %reduce-scatter.17.cloned.1.call-done = bf16[16,4,32,256]{3,2,1,0:T(8,128)(2,1)} async-done(((bf16[16,4,256,256]{3,2,1,0:T(8,128)(2,1)}), bf16[16,4,32,256]{3,2,1,0:T(8,128)(2,1)}) %reduce-scatter.17.cloned.1.call-update) | async-done | bytes 1048592 | tf_op jit(solution)/shard_map/reduce_scatter | solution.py:70
  599.0 2.8 convert_multiply_fusion
  (70 shorter events, 10.1 us)
Async XLA Ops:
  7.2 2.5 copy-start.3
  7.2 28.3 %all-gather.5.cloned.1.call-start = ((), (), s32[]{:S(2)}) async-start(), calls=%async_computation.6 | async-start | bytes 2621440 | tf_op jit(solution)/shard_map/all_gather | solution.py:36
  9.6 50.6 %all-gather.9.cloned.1.call-start = ((), (), s32[]{:S(2)}) async-start(), calls=%async_computation.10 | async-start | bytes 2621440 | tf_op jit(solution)/shard_map/all_gather | solution.py:47
  10.8 2.2 copy-start.4
  10.8 2.5 copy-start.5
  10.8 109.4 %all-gather.7.cloned.1.call-start = ((), (), s32[]{:S(2)}) async-start(), calls=%async_computation.8 | async-start | bytes 2621440 | tf_op jit(solution)/shard_map/all_gather | solution.py:36
  11.9 117.0 %all-gather.11.cloned.1.call-start = ((), (), s32[]{:S(2)}) async-start(), calls=%async_computation.12 | async-start | bytes 2621440 | tf_op jit(solution)/shard_map/all_gather | solution.py:47
  12.9 323.8 %reduce-scatter.11.cloned.1.call-start = ((), (), s32[]{:S(2)}) async-start(), calls=%async_computation.11 | async-start | bytes 2621440 | tf_op jit(solution)/shard_map/reduce_scatter | solution.py:61
  71.5 6.1 copy-start.1
  71.5 12.9 %slice-start = ((s8[8388608]{0:T(1024)(128)(4,1)}), s8[4194304]{0:T(1024)(128)(4,1)S(1)}, s32[]{:S(2)}) async-start(s8[8388608]{0:T(1024)(128)(4,1)} %bitcast.180), calls=%async_computation.16 | async-start | bytes 8388608
  77.6 6.8 %slice-start.1 = ((s8[8388608]{0:T(1024)(128)(4,1)}), s8[4194304]{0:T(1024)(128)(4,1)S(1)}, s32[]{:S(2)}) async-start(s8[8388608]{0:T(1024)(128)(4,1)} %bitcast.180), calls=%async_computation.17 | async-start | bytes 8388608
  119.9 216.8 %reduce-scatter.13.cloned.1.call-start = ((), (), s32[]{:S(2)}) async-start(), calls=%async_computation.13 | async-start | bytes 2621440 | tf_op jit(solution)/shard_map/reduce_scatter | solution.py:61
  137.3 14.8 %slice-start.2 = ((s8[8388608]{0:T(1024)(128)(4,1)}), s8[4194304]{0:T(1024)(128)(4,1)S(1)}, s32[]{:S(2)}) async-start(s8[8388608]{0:T(1024)(128)(4,1)} %bitcast.182), calls=%async_computation.18 | async-start | bytes 8388608
  143.4 8.7 %copy-start = (f32[16,128,256,1]{2,1,3,0:T(8,128)}, f32[16,128,256,1]{2,1,3,0:T(8,128)S(1)}, u32[]{:S(2)}) copy-start(f32[16,128,256,1]{2,1,3,0:T(8,128)S(1)} %fusion.46) | copy-start | bytes 6291460
  143.4 8.7 %slice-start.3 = ((s8[8388608]{0:T(1024)(128)(4,1)}), s8[4194304]{0:T(1024)(128)(4,1)S(1)}, s32[]{:S(2)}) async-start(s8[8388608]{0:T(1024)(128)(4,1)} %bitcast.182), calls=%async_computation.19 | async-start | bytes 8388608
  152.1 6.1 copy-start.2
  187.1 152.4 %reduce-scatter.7.cloned.1.call-start = ((), (), s32[]{:S(2)}) async-start(), calls=%async_computation.7 | async-start | bytes 2621440 | tf_op jit(solution)/shard_map/reduce_scatter | solution.py:43
  225.1 114.4 %reduce-scatter.9.cloned.1.call-start = ((), (), s32[]{:S(2)}) async-start(), calls=%async_computation.9 | async-start | bytes 2621440 | tf_op jit(solution)/shard_map/reduce_scatter | solution.py:43
  263.4 185.2 %reduce-scatter.15.cloned.1.call-start = ((), (), s32[]{:S(2)}) async-start(), calls=%async_computation.14 | async-start | bytes 9437184 | tf_op jit(solution)/shard_map/reduce_scatter | solution.py:67
  299.7 299.3 %reduce-scatter.17.cloned.1.call-start = ((), (), s32[]{:S(2)}) async-start(), calls=%async_computation.15 | async-start | bytes 9437184 | tf_op jit(solution)/shard_map/reduce_scatter | solution.py:70
Sparse Core Ops, SparseCore 0:
  10.1 25.2 all-gather.4
  37.6 22.5 all-gather.8
  62.3 22.5 all-gather.6
  86.9 22.5 all-gather.10
  120.0 31.1 reduce-scatter.10
  187.2 31.0 reduce-scatter.12
  225.2 31.5 reduce-scatter.6
  263.5 31.9 reduce-scatter.8
  299.8 148.6 reduce-scatter.14
  452.0 146.8 reduce-scatter.16
where the time goes:
time: 618 us; the launch traced here: 609 us
  waiting for transfers between devices  297 us (48%)
  matrix products  104 us (17%)
  other arithmetic  98.8 us (16%)
  local copies, waits for them, and re-layouts  92.7 us (15%)
  between operations  14.9 us (2%)
    reduce_scatter x1, waiting for transfers between devices, shards(): lax.psum_scatter(grad_out.astype(jnp.bfloat16), 'dp', scatter_dimension=2...  148 us
    reduce_scatter x1, waiting for transfers between devices, shards(): lax.psum_scatter(grad_in.astype(jnp.bfloat16), 'dp', scatter_dimension=2,...  106 us
    scatter-add x4, other arithmetic, place_blocks(): jnp.zeros((step_tok, row_blocks, side), jnp.float32)  75.1 us
    dot_general x2, matrix products, shards(): jnp.einsum('tjb,tjkc->jkbc', act, picked, preferred_element_type=jnp.floa...  23.8 us
    dot_general x2, matrix products, shards(): jnp.einsum('tjkb,tjc->jkbc', selected, d_pre, preferred_element_type=jnp....  23.3 us
    all_gather x2, waiting for transfers between devices, shards(): x_full = lax.all_gather(x_part, 'mp', axis=1, tiled=True)  21.9 us
    gather x4, local copies, waits for them, and re-layouts, shards(): picked = dy_full.reshape(step_tok, row_blocks, side)[:, out_blocks]  21.7 us
    all_gather x2, waiting for transfers between devices, shards(): dy_full = lax.all_gather(dy_part, 'mp', axis=1, tiled=True)  21.5 us
  transfers between devices with their start and end apart: 10, of which 4 were waited for; matrix products, arithmetic and copies ran while one was open for 48% of the time, Pallas kernels for 0%

commit v1 on v0

--- a/solution.py
+++ b/solution.py
@@ -1,11 +1,18 @@
+import functools
 import math
 
 import jax
 import jax.numpy as jnp
 from jax import lax
+from jax.experimental import pallas as pl
+from jax.experimental.pallas import tpu as pltpu
 from jax.sharding import PartitionSpec as P
 
 MB = 2
+MASKS = (0, 1, 2, 4)
+MESH = pl.DeviceIdType.MESH
+C0 = math.sqrt(2.0 / math.pi)
+C1 = 0.044715
 
 
 def place_blocks(values, targets, row_blocks):
@@ -18,7 +25,7 @@
     return placed.reshape(step_tok, row_blocks * side)
 
 
-def shards(tokens, cotangent, w_in, w_out, in_blocks, out_blocks):
+def shards_plain(tokens, cotangent, w_in, w_out, in_blocks, out_blocks):
     hb_dev, kk, side, _ = w_in.shape
     total_tok = tokens.shape[0]
     width = tokens.shape[1] * lax.axis_size("mp")
@@ -76,7 +83,314 @@
     return (output, grad_tokens, in_share * scale, out_share * scale)
 
 
+def flip(u, m):
+    if m == 0:
+        return u
+    return u + m * (1 - 2 * ((u // m) % 2))
+
+
+def dot(a, b, dims):
+    return lax.dot_general(a, b, (dims, ((), ())), preferred_element_type=jnp.float32)
+
+
+def fused_kernel(
+    dims,
+    in_idx, out_idx, in_inv, out_inv, x_hbm, dy_hbm, win_hbm, wout_hbm,
+    part, red,
+    full, grads, arrived, act, dpre, wbuf, acc, csend, crecv,
+    own_sem, y_send, y_recv, c_send, c_recv, f_send, f_recv,
+    w_sem, g_send, g_recv, z_send, z_recv, zl_sem,
+    o_send, o_recv, p_send, p_recv, pl_sem,
+):
+    ndp, nmp, hb, side, own, tok, rows = dims
+    nz = ndp // 2
+    dp = lax.axis_index("dp")
+    mp = lax.axis_index("mp")
+    z, mx = dp // 2, dp % 2
+    y, core = mp // 2, mp % 2
+    other_core = (dp, y * 2 + 1 - core)
+    other_y = (dp, (1 - y) * 2 + core)
+    other_x = (z * 2 + 1 - mx, mp)
+    g_core = other_core[1]
+    g_y = other_y[1]
+    g_far = (1 - y) * 2 + 1 - core
+    srcs = (x_hbm, dy_hbm)
+
+    def z_peer(dz):
+        return (z + dz) % nz
+
+    barrier = pltpu.get_barrier_semaphore()
+    peers = [other_core, other_y, other_x] + [(z_peer(dz) * 2 + mx, mp) for dz in range(1, nz)]
+    for peer in peers:
+        pl.semaphore_signal(barrier, inc=1, device_id=peer, device_id_type=MESH)
+    pl.semaphore_wait(barrier, len(peers))
+
+    def remote(src, dst, ssem, rsem, peer):
+        return pltpu.make_async_remote_copy(
+            src_ref=src, dst_ref=dst, send_sem=ssem, recv_sem=rsem,
+            device_id=peer, device_id_type=MESH,
+        )
+
+    def piece(a, i):
+        return srcs[a].at[:, pl.ds(pl.multiple_of(i * side, side), side)]
+
+    def to_y(a, i, slot):
+        return remote(piece(a, i), full.at[a, slot * own + i], y_send.at[a, i], y_recv.at[a, i], other_y)
+
+    def to_core(a, i, slot):
+        return remote(piece(a, i), full.at[a, slot * own + i], c_send.at[a, i], c_recv.at[a, i], other_core)
+
+    def forward(a, i, slot):
+        return remote(
+            full.at[a, g_y * own + i], full.at[a, slot * own + i],
+            f_send.at[a, i], f_recv.at[a, i], other_core,
+        )
+
+    def keep(a, i):
+        return pltpu.make_async_copy(piece(a, i), full.at[a, mp * own + i], own_sem.at[a, i])
+
+    def w_copies(j, slot):
+        return (
+            pltpu.make_async_copy(win_hbm.at[j], wbuf.at[slot, 0], w_sem.at[slot, 0, 0]),
+            pltpu.make_async_copy(wout_hbm.at[j], wbuf.at[slot, 1], w_sem.at[slot, 1, 0]),
+        )
+
+    def loop(n, body):
+        lax.fori_loop(0, n, lambda i, c: (body(i), c)[1], 0)
+
+    for a in range(2):
+        def start(i, a=a):
+            to_y(a, i, mp).start()
+            to_core(a, i, mp).start()
+            keep(a, i).start()
+        loop(own, start)
+    for cp in w_copies(0, 0):
+        cp.start()
+    for a in range(2):
+        def relay(i, a=a):
+            to_y(a, i, g_y).wait_recv()
+            forward(a, i, g_y).start()
+        loop(own, relay)
+    for a in range(2):
+        def settle(i, a=a):
+            keep(a, i).wait()
+            to_core(a, i, g_core).wait_recv()
+            forward(a, i, g_far).wait_recv()
+        loop(own, settle)
+
+    def hidden(j):
+        slot = j % 2
+        for cp in w_copies(j, slot):
+            cp.wait()
+
+        @pl.when(j + 1 < hb)
+        def _():
+            for cp in w_copies(j + 1, 1 - slot):
+                cp.start()
+
+        pre = jnp.zeros((tok, side), jnp.float32)
+        d_act = jnp.zeros((tok, side), jnp.float32)
+        for k in range(len(MASKS)):
+            pre += dot(full[0, in_idx[j, k]], wbuf[slot, 0, k], ((1,), (0,)))
+            d_act += dot(full[1, out_idx[j, k]], wbuf[slot, 1, k], ((1,), (1,)))
+        th = jnp.tanh(C0 * (pre + C1 * (pre * pre * pre)))
+        half = 0.5 * (1.0 + th)
+        slope = half + 0.5 * pre * (1.0 - th * th) * (C0 * (1.0 + 3.0 * C1 * pre * pre))
+        act[j] = (pre * half).astype(jnp.bfloat16)
+        dpre[j] = (d_act * slope).astype(jnp.bfloat16)
+
+    loop(hb, hidden)
+
+    def to_x(j):
+        return remote(grads.at[j, 1 - mx], arrived.at[j], g_send.at[j], g_recv.at[j], other_x)
+
+    def weight_grads(j):
+        for k in range(len(MASKS)):
+            gi = dot(full[0, in_idx[j, k]], dpre[j], ((0,), (0,)))
+            go = dot(act[j], full[1, out_idx[j, k]], ((0,), (0,)))
+            for a, value in ((0, gi), (1, go)):
+                value = value.astype(jnp.bfloat16).reshape(nz, 2, rows, side)
+                for xx in range(2):
+                    grads[j, xx, a, k] = value[:, xx]
+        to_x(j).start()
+
+    loop(hb, weight_grads)
+
+    def v_copies(u, slot):
+        res = []
+        for k, m in enumerate(MASKS):
+            v = flip(u, m)
+            res.append(pltpu.make_async_copy(win_hbm.at[v, k], wbuf.at[slot, 0, k], w_sem.at[slot, 0, k]))
+            res.append(pltpu.make_async_copy(wout_hbm.at[v, k], wbuf.at[slot, 1, k], w_sem.at[slot, 1, k]))
+        return res
+
+    for cp in v_copies(0, 0):
+        cp.start()
+
+    def place(u):
+        slot = u % 2
+        for cp in v_copies(u, slot):
+            cp.wait()
+
+        @pl.when(u + 1 < hb)
+        def _():
+            for cp in v_copies(u + 1, 1 - slot):
+                cp.start()
+
+        out = jnp.zeros((tok, side), jnp.float32)
+        back = jnp.zeros((tok, side), jnp.float32)
+        for k, m in enumerate(MASKS):
+            v = flip(u, m)
+            out += dot(act[v], wbuf[slot, 1, k], ((1,), (0,)))
+            back += dot(dpre[v], wbuf[slot, 0, k], ((1,), (1,)))
+        acc[0, u] = out.astype(jnp.bfloat16)
+        acc[1, u] = back.astype(jnp.bfloat16)
+
+    loop(hb, place)
+    inv = (out_inv, in_inv)
+    for a in range(2):
+        acc[a, hb] = jnp.zeros((tok, side), jnp.bfloat16)
+
+    def swap(a):
+        return remote(csend.at[a], crecv.at[a], o_send.at[a], o_recv.at[a], other_core)
+
+    for a in range(2):
+        for yy in range(2):
+            def fill(i, a=a, yy=yy):
+                csend[a, yy, i] = acc[a, inv[a][(2 * yy + 1 - core) * own + i]]
+            loop(own, fill)
+        swap(a).start()
+
+    def to_part(a):
+        return remote(crecv.at[a, 1 - y], part.at[a, 1], p_send.at[a], p_recv.at[a], other_y)
+
+    def keep_part(a):
+        return pltpu.make_async_copy(crecv.at[a, y], part.at[a, 0], pl_sem.at[a])
+
+    for a in range(2):
+        swap(a).wait_recv()
+        for yy in range(2):
+            def join(i, a=a, yy=yy):
+                crecv[a, yy, i] = crecv[a, yy, i] + acc[a, inv[a][(2 * yy + core) * own + i]]
+            loop(own, join)
+        to_part(a).start()
+        keep_part(a).start()
+
+    def to_z(j, dz, slot):
+        return remote(
+            grads.at[j, mx, :, :, z_peer(dz)], red.at[slot, :, j],
+            z_send.at[dz - 1, j], z_recv.at[dz - 1, j], (z_peer(dz) * 2 + mx, mp),
+        )
+
+    def keep_z(j):
+        return pltpu.make_async_copy(grads.at[j, mx, :, :, z], red.at[z, :, j], zl_sem.at[j])
+
+    def pair_sum(j):
+        to_x(j).wait_recv()
+        for a in range(2):
+            for k in range(len(MASKS)):
+                grads[j, mx, a, k] = (
+                    grads[j, mx, a, k].astype(jnp.float32) + arrived[j, a, k].astype(jnp.float32)
+                ).astype(jnp.bfloat16)
+        for dz in range(1, nz):
+            to_z(j, dz, z).start()
+        keep_z(j).start()
+
+    loop(hb, pair_sum)
+
+    for a in range(2):
+        def drain(i, a=a):
+            to_y(a, i, mp).wait_send()
+            to_core(a, i, mp).wait_send()
+            forward(a, i, g_y).wait_send()
+        loop(own, drain)
+        swap(a).wait_send()
+        to_part(a).wait_send()
+        to_part(a).wait_recv()
+        keep_part(a).wait()
+
+    def finish(j):
+        to_x(j).wait_send()
+        keep_z(j).wait()
+        for dz in range(1, nz):
+            to_z(j, dz, z).wait_send()
+            to_z(j, dz, (z - dz + nz) % nz).wait_recv()
+
+    loop(hb, finish)
+
+
+def shards_fused(ndp, nmp, tokens, cotangent, w_in, w_out, in_blocks, out_blocks):
+    hb, kk, side, _ = w_in.shape
+    tok, feats = tokens.shape
+    own = feats // side
+    blocks = own * nmp
+    nz = ndp // 2
+    rows = side // ndp
+
+    def inverse(table):
+        hit = table[:, 0][None, :] == jnp.arange(blocks, dtype=jnp.int32)[:, None]
+        where = jnp.sum(jnp.where(hit, jnp.arange(hb, dtype=jnp.int32)[None, :], 0), axis=1)
+        return jnp.where(jnp.any(hit, axis=1), where, hb).astype(jnp.int32)
+
+    bf = jnp.bfloat16
+    any_spec = pl.BlockSpec(memory_space=pl.ANY)
+    smem = pl.BlockSpec(memory_space=pltpu.SMEM)
+    dma = pltpu.SemaphoreType.DMA
+    part, red = pl.pallas_call(
+        functools.partial(fused_kernel, (ndp, nmp, hb, side, own, tok, rows)),
+        out_shape=(
+            jax.ShapeDtypeStruct((2, 2, own, tok, side), bf),
+            jax.ShapeDtypeStruct((nz, 2, hb, kk, rows, side), bf),
+        ),
+        in_specs=[smem] * 4 + [any_spec] * 4,
+        out_specs=(any_spec, any_spec),
+        scratch_shapes=[
+            pltpu.VMEM((2, blocks, tok, side), bf),
+            pltpu.VMEM((hb, 2, 2, kk, nz, rows, side), bf),
+            pltpu.VMEM((hb, 2, kk, nz, rows, side), bf),
+            pltpu.VMEM((hb, tok, side), bf),
+            pltpu.VMEM((hb, tok, side), bf),
+            pltpu.VMEM((2, 2, kk, side, side), bf),
+            pltpu.VMEM((2, hb + 1, tok, side), bf),
+            pltpu.VMEM((2, 2, own, tok, side), bf),
+            pltpu.VMEM((2, 2, own, tok, side), bf),
+        ]
+        + [dma((2, own))] * 7
+        + [dma((2, 2, kk)), dma((hb,)), dma((hb,)), dma((nz - 1, hb)), dma((nz - 1, hb)), dma((hb,))]
+        + [dma((2,))] * 5,
+        compiler_params=pltpu.CompilerParams(
+            collective_id=0, has_side_effects=True, vmem_limit_bytes=66_000_000
+        ),
+    )(
+        in_blocks, out_blocks, inverse(in_blocks), inverse(out_blocks),
+        tokens, cotangent, w_in, w_out,
+    )
+    scale = 1.0 / math.sqrt(tok * ndp)
+    both = part[:, 0].astype(jnp.float32) + part[:, 1].astype(jnp.float32)
+    both = both.astype(bf).transpose(0, 2, 1, 3).reshape(2, tok, feats)
+    total = red.astype(jnp.float32).sum(axis=0) * scale
+    return both[0], both[1], total[0], total[1]
+
+
 def solution(mesh):
+    ndp, nmp = mesh.shape["dp"], mesh.shape["mp"]
+
+    def shards(tokens, cotangent, w_in, w_out, in_blocks, out_blocks):
+        hb, kk, side, _ = w_in.shape
+        blocks = tokens.shape[1] * nmp // side
+        fits = (
+            nmp == 4
+            and ndp % 2 == 0
+            and kk == len(MASKS)
+            and 2 * hb == blocks
+            and hb % 8 == 0
+            and side % (16 * ndp) == 0
+        )
+        args = (tokens, cotangent, w_in, w_out, in_blocks, out_blocks)
+        if fits:
+            return shards_fused(ndp, nmp, *args)
+        return shards_plain(*args)
+
     placed = (
         P("dp", "mp"),
         P("dp", "mp"),

time: 618 us -> 314 us (0.51); the launches traced: 609 us -> 313 us
  waiting for transfers between devices: 297 us -> 0 us
  Pallas kernels: 0 us -> 291 us
  matrix products: 104 us -> 0 us
  other arithmetic: 98.8 us -> 10.6 us
  local copies, waits for them, and re-layouts: 92.7 us -> 10.5 us
  between operations: 14.9 us -> 0.69 us
    pallas_call x0 -> x1, Pallas kernels: none -> 291 us  [shards_fused(): pl.pallas_call(functools.partial(fused_kernel, (ndp, nmp, hb, side, own,...]
    reduce_scatter x6 -> x0, waiting for transfers between devices: 254 us -> none  [the longest x1 148 us: shards(): lax.psum_scatter(grad_out.astype(jnp.bfloat16), 'dp', scatter_dimension=2...]
    dot_general x12 -> x0, matrix products: 104 us -> none  [the longest x2 23.8 us: shards(): jnp.einsum('tjb,tjkc->jkbc', act, picked, preferred_element_type=jnp.floa...]
    scatter-add x4 -> x0, other arithmetic: 75.1 us -> none  [place_blocks(): jnp.zeros((step_tok, row_blocks, side), jnp.float32)]
    all_gather x4 -> x0, waiting for transfers between devices: 43.3 us -> none  [the longest x2 21.9 us: shards(): x_full = lax.all_gather(x_part, 'mp', axis=1, tiled=True)]
    gather x8 -> x0, local copies, waits for them, and re-layouts: 42.1 us -> none  [the longest x4 21.7 us: shards(): picked = dy_full.reshape(step_tok, row_blocks, side)[:, out_blocks]]
    convert_element_type x4 -> x0, local copies, waits for them, and re-layouts: 16.3 us -> none  [the longest x2 8.16 us: shards(): partial_back.astype(jnp.bfloat16)]
    reshape x6 -> x0, local copies, waits for them, and re-layouts: 15.7 us -> none  [the longest x2 8.16 us: shards(): picked = dy_full.reshape(step_tok, row_blocks, side)[:, out_blocks]]
  transfers between devices with their start and end apart: 10 -> 0, of which waited for: 4 -> 0; matrix products, arithmetic and copies ran while one was open for 48% -> 0% of each run, Pallas kernels for 0% -> 0%
where the time goes in v1:
time: 314 us; the launch traced here: 313 us
  Pallas kernels  291 us (93%)
  other arithmetic  10.6 us (3%)
  local copies, waits for them, and re-layouts  10.5 us (3%)
    pallas_call x1, Pallas kernels, shards_fused(): pl.pallas_call(functools.partial(fused_kernel, (ndp, nmp, hb, side, own,...  291 us

profile of v1, /device:TPU:0, one launch (start us, length us, event | category | flops | bytes accessed | tf_op | source)
XLA Modules:
  0.0 312.6 jit_solution(13506720367293295103)
XLA Ops:
  0.6 0.7 slice_bitcast_fusion.3
  1.3 0.7 slice_bitcast_fusion.2
  2.0 0.1 select_reduce_fusion
  2.1 0.1 fusion.1
  2.2 0.1 select_reduce_fusion.1
  2.3 0.1 fusion.2
  2.4 0.5 broadcast_select_fusion
  2.9 1.4 copy.18.in_idx
  4.2 1.4 copy.19.out_idx
  5.6 290.8 %shard_map.93 = (bf16[2,2,8,256,256]{4,3,2,1,0:T(8,128)(2,1)}, bf16[4,2,16,4,32,256]{5,4,3,2,1,0:T(8,128)(2,1)}) custom-call(s32[16,4]{1,0:T(8,128)} %copy.18.in_idx, s32[16,4]{1,0:T(8,128)} %copy.19.out_idx, s32[32]{0:T(128)} %get-tuple-element.21.in_inv, s32[32]{0:T(128)} %get-tuple-element.20.out_inv, bf16[256,2048]{1,0:T(8,128)(2,1)} %x_hbm.1, ...), custom_call_target="tpu_custom_call" | custom-call | tf_op jit(solution)/shard_map/pallas_call | solution.py:339
  296.4 2.9 fusion
  299.3 0.2 fusion.3
  299.5 0.5 copy.21
  300.0 1.4 copy.23
  301.4 0.5 copy.20
  301.9 1.4 copy.22
  303.4 6.0 %convert_reduce_fusion = f32[2,16,4,32,256]{4,3,2,1,0:T(8,128)S(1)} fusion(bf16[4,2,16,4,32,256]{5,4,3,2,1,0:T(8,128)(2,1)} %get-tuple-element.7), kind=kLoop, calls=%fused_computation | loop fusion | flops 7340032 | bytes 12582912 | tf_op jit(solution)/shard_map/reduce_sum | solution.py:371
  309.3 0.9 broadcast_multiply_fusion
  310.3 2.3 slice_bitcast_fusion

commit v2 on v1

--- a/solution.py
+++ b/solution.py
@@ -13,6 +13,7 @@
 MESH = pl.DeviceIdType.MESH
 C0 = math.sqrt(2.0 / math.pi)
 C1 = 0.044715
+SKEW = 2
 
 
 def place_blocks(values, targets, row_blocks):
@@ -96,13 +97,15 @@
 def fused_kernel(
     dims,
     in_idx, out_idx, in_inv, out_inv, x_hbm, dy_hbm, win_hbm, wout_hbm,
-    part, red,
-    full, grads, arrived, act, dpre, wbuf, acc, csend, crecv,
+    part_out, part_back, red,
+    full, near, mine, theirs, arrived, act, dpre, act2, dpre2, wbuf, acc, csend, crecv, zbuf,
     own_sem, y_send, y_recv, c_send, c_recv, f_send, f_recv,
-    w_sem, g_send, g_recv, z_send, z_recv, zl_sem,
-    o_send, o_recv, p_send, p_recv, pl_sem,
+    x_send, x_recv, y2_send, y2_recv, c2_send, c2_recv, f2_send, f2_recv,
+    p_send, p_recv, pl_sem,
+    w_sem, g_send, g_recv, up_send, up_recv, dn_send, dn_recv, zl_sem,
+    o_send, o_recv,
 ):
-    ndp, nmp, hb, side, own, tok, rows = dims
+    ndp, nmp, hb, side, own, tok, rows, n1 = dims
     nz = ndp // 2
     dp = lax.axis_index("dp")
     mp = lax.axis_index("mp")
@@ -111,16 +114,19 @@
     other_core = (dp, y * 2 + 1 - core)
     other_y = (dp, (1 - y) * 2 + core)
     other_x = (z * 2 + 1 - mx, mp)
+    above = ((dp + 2) % ndp, mp)
+    below = ((dp + ndp - 2) % ndp, mp)
+    has_above = z < nz - 1
+    has_below = z > 0
     g_core = other_core[1]
     g_y = other_y[1]
     g_far = (1 - y) * 2 + 1 - core
     srcs = (x_hbm, dy_hbm)
-
-    def z_peer(dz):
-        return (z + dz) % nz
+    parts = (part_out, part_back)
+    nk = len(MASKS)
 
     barrier = pltpu.get_barrier_semaphore()
-    peers = [other_core, other_y, other_x] + [(z_peer(dz) * 2 + mx, mp) for dz in range(1, nz)]
+    peers = [other_core, other_y, other_x] + [((dp + 2 * dz) % ndp, mp) for dz in range(1, nz)]
     for peer in peers:
         pl.semaphore_signal(barrier, inc=1, device_id=peer, device_id_type=MESH)
     pl.semaphore_wait(barrier, len(peers))
@@ -131,8 +137,11 @@
             device_id=peer, device_id_type=MESH,
         )
 
+    def lanes(i):
+        return pl.ds(pl.multiple_of(i * side, side), side)
+
     def piece(a, i):
-        return srcs[a].at[:, pl.ds(pl.multiple_of(i * side, side), side)]
+        return srcs[a].at[:, lanes(i)]
 
     def to_y(a, i, slot):
         return remote(piece(a, i), full.at[a, slot * own + i], y_send.at[a, i], y_recv.at[a, i], other_y)
@@ -146,6 +155,27 @@
             f_send.at[a, i], f_recv.at[a, i], other_core,
         )
 
+    def to_near(a, i):
+        return remote(piece(a, i), near.at[a, mp * own + i], x_send.at[a, i], x_recv.at[a, i], other_x)
+
+    def near_y(a, i, slot):
+        return remote(
+            near.at[a, mp * own + i], near.at[a, slot * own + i],
+            y2_send.at[a, i], y2_recv.at[a, i], other_y,
+        )
+
+    def near_core(a, i, slot):
+        return remote(
+            near.at[a, mp * own + i], near.at[a, slot * own + i],
+            c2_send.at[a, i], c2_recv.at[a, i], other_core,
+        )
+
+    def near_forward(a, i, slot):
+        return remote(
+            near.at[a, g_y * own + i], near.at[a, slot * own + i],
+            f2_send.at[a, i], f2_recv.at[a, i], other_core,
+        )
+
     def keep(a, i):
         return pltpu.make_async_copy(piece(a, i), full.at[a, mp * own + i], own_sem.at[a, i])
 
@@ -155,12 +185,13 @@
             pltpu.make_async_copy(wout_hbm.at[j], wbuf.at[slot, 1], w_sem.at[slot, 1, 0]),
         )
 
-    def loop(n, body):
-        lax.fori_loop(0, n, lambda i, c: (body(i), c)[1], 0)
+    def loop(n, body, first=0):
+        lax.fori_loop(first, n, lambda i, c: (body(i), c)[1], 0)
 
     for a in range(2):
         def start(i, a=a):
             to_y(a, i, mp).start()
+            to_near(a, i).start()
             to_core(a, i, mp).start()
             keep(a, i).start()
         loop(own, start)
@@ -170,6 +201,9 @@
         def relay(i, a=a):
             to_y(a, i, g_y).wait_recv()
             forward(a, i, g_y).start()
+            to_near(a, i).wait_recv()
+            near_y(a, i, mp).start()
+            near_core(a, i, mp).start()
         loop(own, relay)
     for a in range(2):
         def settle(i, a=a):
@@ -178,43 +212,51 @@
             forward(a, i, g_far).wait_recv()
         loop(own, settle)
 
-    def hidden(j):
-        slot = j % 2
-        for cp in w_copies(j, slot):
-            cp.wait()
-
-        @pl.when(j + 1 < hb)
-        def _():
-            for cp in w_copies(j + 1, 1 - slot):
-                cp.start()
-
-        pre = jnp.zeros((tok, side), jnp.float32)
-        d_act = jnp.zeros((tok, side), jnp.float32)
-        for k in range(len(MASKS)):
-            pre += dot(full[0, in_idx[j, k]], wbuf[slot, 0, k], ((1,), (0,)))
-            d_act += dot(full[1, out_idx[j, k]], wbuf[slot, 1, k], ((1,), (1,)))
-        th = jnp.tanh(C0 * (pre + C1 * (pre * pre * pre)))
-        half = 0.5 * (1.0 + th)
-        slope = half + 0.5 * pre * (1.0 - th * th) * (C0 * (1.0 + 3.0 * C1 * pre * pre))
-        act[j] = (pre * half).astype(jnp.bfloat16)
-        dpre[j] = (d_act * slope).astype(jnp.bfloat16)
-
-    loop(hb, hidden)
+    def hidden_of(source, act_ref, dpre_ref):
+        def hidden(j):
+            slot = j % 2
+            for cp in w_copies(j, slot):
+                cp.wait()
+
+            @pl.when(j + 1 < hb)
+            def _():
+                for cp in w_copies(j + 1, 1 - slot):
+                    cp.start()
+
+            pre = jnp.zeros((tok, side), jnp.float32)
+            d_act = jnp.zeros((tok, side), jnp.float32)
+            for k in range(nk):
+                pre += dot(source[0, in_idx[j, k]], wbuf[slot, 0, k], ((1,), (0,)))
+                d_act += dot(source[1, out_idx[j, k]], wbuf[slot, 1, k], ((1,), (1,)))
+            th = jnp.tanh(C0 * (pre + C1 * (pre * pre * pre)))
+            half = 0.5 * (1.0 + th)
+            slope = half + 0.5 * pre * (1.0 - th * th) * (C0 * (1.0 + 3.0 * C1 * pre * pre))
+            act_ref[j] = (pre * half).astype(jnp.bfloat16)
+            dpre_ref[j] = (d_act * slope).astype(jnp.bfloat16)
+
+        loop(hb, hidden)
+
+    hidden_of(full, act, dpre)
 
     def to_x(j):
-        return remote(grads.at[j, 1 - mx], arrived.at[j], g_send.at[j], g_recv.at[j], other_x)
+        return remote(theirs.at[j], arrived.at[j], g_send.at[j], g_recv.at[j], other_x)
+
+    def split(value):
+        value = value.astype(jnp.bfloat16).reshape(nz, 2, rows, side)
+        low, high = value[:, 0], value[:, 1]
+        return jnp.where(mx == 0, low, high), jnp.where(mx == 0, high, low)
 
     def weight_grads(j):
-        for k in range(len(MASKS)):
+        for k in range(nk):
             gi = dot(full[0, in_idx[j, k]], dpre[j], ((0,), (0,)))
             go = dot(act[j], full[1, out_idx[j, k]], ((0,), (0,)))
             for a, value in ((0, gi), (1, go)):
-                value = value.astype(jnp.bfloat16).reshape(nz, 2, rows, side)
-                for xx in range(2):
-                    grads[j, xx, a, k] = value[:, xx]
+                mine_half, their_half = split(value)
+                mine[j, a, k] = mine_half
+                theirs[j, a, k] = their_half
         to_x(j).start()
 
-    loop(hb, weight_grads)
+    loop(n1, weight_grads)
 
     def v_copies(u, slot):
         res = []
@@ -247,6 +289,8 @@
         acc[1, u] = back.astype(jnp.bfloat16)
 
     loop(hb, place)
+    for cp in w_copies(0, 0):
+        cp.start()
     inv = (out_inv, in_inv)
     for a in range(2):
         acc[a, hb] = jnp.zeros((tok, side), jnp.bfloat16)
@@ -261,11 +305,13 @@
             loop(own, fill)
         swap(a).start()
 
-    def to_part(a):
-        return remote(crecv.at[a, 1 - y], part.at[a, 1], p_send.at[a], p_recv.at[a], other_y)
-
-    def keep_part(a):
-        return pltpu.make_async_copy(crecv.at[a, y], part.at[a, 0], pl_sem.at[a])
+    def to_part(a, i):
+        return remote(
+            crecv.at[a, 1 - y, i], parts[a].at[1, :, lanes(i)], p_send.at[a, i], p_recv.at[a, i], other_y
+        )
+
+    def keep_part(a, i):
+        return pltpu.make_async_copy(crecv.at[a, y, i], parts[a].at[0, :, lanes(i)], pl_sem.at[a, i])
 
     for a in range(2):
         swap(a).wait_recv()
@@ -273,48 +319,142 @@
             def join(i, a=a, yy=yy):
                 crecv[a, yy, i] = crecv[a, yy, i] + acc[a, inv[a][(2 * yy + core) * own + i]]
             loop(own, join)
-        to_part(a).start()
-        keep_part(a).start()
-
-    def to_z(j, dz, slot):
-        return remote(
-            grads.at[j, mx, :, :, z_peer(dz)], red.at[slot, :, j],
-            z_send.at[dz - 1, j], z_recv.at[dz - 1, j], (z_peer(dz) * 2 + mx, mp),
-        )
+
+        def emit(i, a=a):
+            to_part(a, i).start()
+            keep_part(a, i).start()
+        loop(own, emit)
+
+    def up(j, u, last):
+        dst = red.at[1, :, j] if last else zbuf.at[u - 1, j]
+        return remote(mine.at[j, :, :, u], dst, up_send.at[u - 1, j], up_recv.at[u - 1, j], above)
+
+    def down(j, u, last):
+        dst = red.at[2, :, j] if last else zbuf.at[u, j]
+        return remote(mine.at[j, :, :, u], dst, dn_send.at[u, j], dn_recv.at[u, j], below)
 
     def keep_z(j):
-        return pltpu.make_async_copy(grads.at[j, mx, :, :, z], red.at[z, :, j], zl_sem.at[j])
-
-    def pair_sum(j):
-        to_x(j).wait_recv()
+        return pltpu.make_async_copy(mine.at[j, :, :, z], red.at[0, :, j], zl_sem.at[j])
+
+    def add_in(j, u, slot):
         for a in range(2):
-            for k in range(len(MASKS)):
-                grads[j, mx, a, k] = (
-                    grads[j, mx, a, k].astype(jnp.float32) + arrived[j, a, k].astype(jnp.float32)
+            mine[j, a, :, u] = (
+                mine[j, a, :, u].astype(jnp.float32) + zbuf[slot, j, a].astype(jnp.float32)
+            ).astype(jnp.bfloat16)
+
+    def hops(t):
+        ju = t - SKEW * z
+        jd = t - SKEW * (nz - 1 - z)
+        up_ok = jnp.logical_and(ju >= 0, ju < hb)
+        dn_ok = jnp.logical_and(jd >= 0, jd < hb)
+        for u in range(nz - 1, 0, -1):
+            @pl.when(jnp.logical_and(up_ok, z < u))
+            def _(u=u):
+                @pl.when(has_below)
+                def _():
+                    up(ju, u, False).wait_recv()
+                    add_in(ju, u, u - 1)
+
+                @pl.when(z == u - 1)
+                def _():
+                    up(ju, u, True).start()
+
+                @pl.when(z < u - 1)
+                def _():
+                    up(ju, u, False).start()
+        for u in range(nz - 1):
+            @pl.when(jnp.logical_and(dn_ok, z > u))
+            def _(u=u):
+                @pl.when(has_above)
+                def _():
+                    down(jd, u, False).wait_recv()
+                    add_in(jd, u, u)
+
+                @pl.when(z == u + 1)
+                def _():
+                    down(jd, u, True).start()
+
+                @pl.when(z > u + 1)
+                def _():
+                    down(jd, u, False).start()
+
+    def first_steps(t):
+        to_x(t).wait_recv()
+        for a in range(2):
+            for k in range(nk):
+                mine[t, a, k] = (
+                    mine[t, a, k].astype(jnp.float32) + arrived[t, a, k].astype(jnp.float32)
                 ).astype(jnp.bfloat16)
-        for dz in range(1, nz):
-            to_z(j, dz, z).start()
-        keep_z(j).start()
-
-    loop(hb, pair_sum)
+        keep_z(t).start()
+        hops(t)
+
+    loop(n1, first_steps)
+
+    for a in range(2):
+        def relay2(i, a=a):
+            near_y(a, i, g_y).wait_recv()
+            near_forward(a, i, g_y).start()
+        loop(own, relay2)
+    for a in range(2):
+        def settle2(i, a=a):
+            near_core(a, i, g_core).wait_recv()
+            near_forward(a, i, g_far).wait_recv()
+        loop(own, settle2)
+
+    hidden_of(near, act2, dpre2)
+
+    def later_steps(t):
+        for k in range(nk):
+            gi = dot(full[0, in_idx[t, k]], dpre[t], ((0,), (0,)))
+            gi += dot(near[0, in_idx[t, k]], dpre2[t], ((0,), (0,)))
+            go = dot(act[t], full[1, out_idx[t, k]], ((0,), (0,)))
+            go += dot(act2[t], near[1, out_idx[t, k]], ((0,), (0,)))
+            mine[t, 0, k] = split(gi)[0]
+            mine[t, 1, k] = split(go)[0]
+        keep_z(t).start()
+        hops(t)
+
+    loop(hb, later_steps, n1)
+    loop(hb + SKEW * (nz - 2), hops, hb)
 
     for a in range(2):
         def drain(i, a=a):
             to_y(a, i, mp).wait_send()
             to_core(a, i, mp).wait_send()
             forward(a, i, g_y).wait_send()
+            to_near(a, i).wait_send()
+            near_y(a, i, mp).wait_send()
+            near_core(a, i, mp).wait_send()
+            near_forward(a, i, g_y).wait_send()
+            to_part(a, i).wait_send()
+            to_part(a, i).wait_recv()
+            keep_part(a, i).wait()
         loop(own, drain)
         swap(a).wait_send()
-        to_part(a).wait_send()
-        to_part(a).wait_recv()
-        keep_part(a).wait()
+
+    def sent(j):
+        to_x(j).wait_send()
+
+    loop(n1, sent)
 
     def finish(j):
-        to_x(j).wait_send()
         keep_z(j).wait()
-        for dz in range(1, nz):
-            to_z(j, dz, z).wait_send()
-            to_z(j, dz, (z - dz + nz) % nz).wait_recv()
+        for u in range(1, nz):
+            @pl.when(z < u)
+            def _(u=u):
+                up(j, u, True).wait_send()
+
+            @pl.when(z == u)
+            def _(u=u):
+                up(j, u, True).wait_recv()
+        for u in range(nz - 1):
+            @pl.when(z > u)
+            def _(u=u):
+                down(j, u, True).wait_send()
+
+            @pl.when(z == u)
+            def _(u=u):
+                down(j, u, True).wait_recv()
 
     loop(hb, finish)
 
@@ -326,6 +466,7 @@
     blocks = own * nmp
     nz = ndp // 2
     rows = side // ndp
+    n1 = hb // 4
 
     def inverse(table):
         hit = table[:, 0][None, :] == jnp.arange(blocks, dtype=jnp.int32)[:, None]
@@ -336,40 +477,56 @@
     any_spec = pl.BlockSpec(memory_space=pl.ANY)
     smem = pl.BlockSpec(memory_space=pltpu.SMEM)
     dma = pltpu.SemaphoreType.DMA
-    part, red = pl.pallas_call(
-        functools.partial(fused_kernel, (ndp, nmp, hb, side, own, tok, rows)),
+    part_out, part_back, red = pl.pallas_call(
+        functools.partial(fused_kernel, (ndp, nmp, hb, side, own, tok, rows, n1)),
         out_shape=(
-            jax.ShapeDtypeStruct((2, 2, own, tok, side), bf),
-            jax.ShapeDtypeStruct((nz, 2, hb, kk, rows, side), bf),
+            jax.ShapeDtypeStruct((2, tok, feats), bf),
+            jax.ShapeDtypeStruct((2, tok, feats), bf),
+            jax.ShapeDtypeStruct((3, 2, hb, kk, rows, side), bf),
         ),
         in_specs=[smem] * 4 + [any_spec] * 4,
-        out_specs=(any_spec, any_spec),
+        out_specs=(any_spec,) * 3,
         scratch_shapes=[
             pltpu.VMEM((2, blocks, tok, side), bf),
-            pltpu.VMEM((hb, 2, 2, kk, nz, rows, side), bf),
+            pltpu.VMEM((2, blocks, tok, side), bf),
             pltpu.VMEM((hb, 2, kk, nz, rows, side), bf),
+            pltpu.VMEM((n1, 2, kk, nz, rows, side), bf),
+            pltpu.VMEM((n1, 2, kk, nz, rows, side), bf),
+            pltpu.VMEM((hb, tok, side), bf),
+            pltpu.VMEM((hb, tok, side), bf),
             pltpu.VMEM((hb, tok, side), bf),
             pltpu.VMEM((hb, tok, side), bf),
             pltpu.VMEM((2, 2, kk, side, side), bf),
             pltpu.VMEM((2, hb + 1, tok, side), bf),
             pltpu.VMEM((2, 2, own, tok, side), bf),
             pltpu.VMEM((2, 2, own, tok, side), bf),
+            pltpu.VMEM((nz - 1, hb, 2, kk, rows, side), bf),
         ]
-        + [dma((2, own))] * 7
-        + [dma((2, 2, kk)), dma((hb,)), dma((hb,)), dma((nz - 1, hb)), dma((nz - 1, hb)), dma((hb,))]
-        + [dma((2,))] * 5,
+        + [dma((2, own))] * 18
+        + [dma((2, 2, kk)), dma((n1,)), dma((n1,))]
+        + [dma((nz - 1, hb))] * 4
+        + [dma((hb,))]
+        + [dma((2,))] * 2,
         compiler_params=pltpu.CompilerParams(
-            collective_id=0, has_side_effects=True, vmem_limit_bytes=66_000_000
+            collective_id=0, has_side_effects=True, vmem_limit_bytes=67_000_000
         ),
     )(
         in_blocks, out_blocks, inverse(in_blocks), inverse(out_blocks),
         tokens, cotangent, w_in, w_out,
     )
     scale = 1.0 / math.sqrt(tok * ndp)
-    both = part[:, 0].astype(jnp.float32) + part[:, 1].astype(jnp.float32)
-    both = both.astype(bf).transpose(0, 2, 1, 3).reshape(2, tok, feats)
-    total = red.astype(jnp.float32).sum(axis=0) * scale
-    return both[0], both[1], total[0], total[1]
+    wide = jnp.float32
+    z = lax.axis_index("dp") // 2
+
+    def both(part):
+        return (part[0].astype(wide) + part[1].astype(wide)).astype(bf)
+
+    def total(a):
+        low = jnp.where(z > 0, red[1, a].astype(wide), 0.0)
+        high = jnp.where(z < nz - 1, red[2, a].astype(wide), 0.0)
+        return (red[0, a].astype(wide) + low + high) * scale
+
+    return both(part_out), both(part_back), total(0), total(1)
 
 
 def solution(mesh):
@@ -381,6 +538,7 @@
         fits = (
             nmp == 4
             and ndp % 2 == 0
+            and ndp > 4
             and kk == len(MASKS)
             and 2 * hb == blocks
             and hb % 8 == 0

time: 314 us -> 275 us (0.88)
  Pallas kernels: 291 us -> 259 us
  local copies, waits for them, and re-layouts: 10.5 us -> 4.08 us
    pallas_call x1, Pallas kernels: 291 us -> 259 us  [shards_fused(): pl.pallas_call(functools.partial(fused_kernel, (ndp, nmp, hb, side, own,...]
    reduce_sum x1 -> x0, other arithmetic: 5.97 us -> none  [shards_fused(): total = red.astype(jnp.float32).sum(axis=0) * scale]
    convert_element_type x0 -> x1, other arithmetic: none -> 4.55 us  [both(): return (part[0].astype(wide) + part[1].astype(wide)).astype(bf)]
where the time goes in v2:
time: 275 us; the launch traced here: 273 us
  Pallas kernels  259 us (94%)
  other arithmetic  9.48 us (3%)
  local copies, waits for them, and re-layouts  4.08 us (1%)
    pallas_call x1, Pallas kernels, shards_fused(): pl.pallas_call(functools.partial(fused_kernel, (ndp, nmp, hb, side, own,...  259 us

profile of v2, /device:TPU:0, one launch (start us, length us, event | category | flops | bytes accessed | tf_op | source)
XLA Modules:
  0.0 273.4 jit_solution(14424049574037472082)
XLA Ops:
  0.6 0.7 slice_bitcast_fusion.1
  1.3 0.7 slice_bitcast_fusion
  2.0 0.1 select_reduce_fusion
  2.1 0.1 fusion.2
  2.2 0.5 broadcast_select_fusion.out_inv
  2.7 0.1 select_reduce_fusion.1
  2.8 0.1 fusion.3
  2.9 0.5 broadcast_select_fusion.1.in_inv
  3.4 1.4 copy.12.in_idx
  4.8 1.4 copy.13.out_idx
  6.1 259.2 %shard_map.93 = (bf16[2,256,2048]{2,1,0:T(8,128)(2,1)}, bf16[2,256,2048]{2,1,0:T(8,128)(2,1)}, bf16[3,2,16,4,32,256]{5,4,3,2,1,0:T(8,128)(2,1)}) custom-call(s32[16,4]{1,0:T(8,128)} %copy.12.in_idx, s32[16,4]{1,0:T(8,128)} %copy.13.out_idx, s32[32]{0:T(128)} %broadcast_select_fusion.1.in_inv, s32[32]{0:T(128)} %broadcast_select_fusion.out_inv, ...), custom_call_target="tpu_custom_call" | custom-call | tf_op jit(solution)/shard_map/pallas_call | solution.py:480
  265.3 0.0 copy-start
  265.3 4.5 %fusion = (bf16[256,2048]{1,0:T(8,128)(2,1)}, bf16[256,2048]{1,0:T(8,128)(2,1)}) fusion(bf16[2,256,2048]{2,1,0:T(8,128)(2,1)} %get-tuple-element.7, bf16[2,256,2048]{2,1,0:T(8,128)(2,1)} %get-tuple-element.8), kind=kLoop, calls=%fused_computation.4 | loop fusion | flops 4194304 | bytes 6291456 | tf_op jit(solution)/shard_map/convert_element_type | solution.py:522
  269.9 0.0 copy-done
  269.9 3.5 %multiply_bitcast_fusion = (f32[16,4,32,256]{3,2,1,0:T(8,128)}, f32[16,4,32,256]{3,2,1,0:T(8,128)}) fusion(bf16[3,2,16,4,32,256]{5,4,3,2,1,0:T(8,128)(2,1)S(1)} %copy-done, pred[]{:T(512)S(6)} %lt.4, pred[]{:T(512)S(6)} %gt.4), kind=kLoop, calls=%fused_computation | loop fusion | flops 8388608 | bytes 10485762 | tf_op jit(solution)/shard_map/mul | solution.py:527
Async XLA Ops:
  265.3 4.6 %copy-start = (bf16[3,2,16,4,32,256]{5,4,3,2,1,0:T(8,128)(2,1)S(1)}, bf16[3,2,16,4,32,256]{5,4,3,2,1,0:T(8,128)(2,1)}, u32[]{:S(2)}) copy-start(bf16[3,2,16,4,32,256]{5,4,3,2,1,0:T(8,128)(2,1)} %get-tuple-element.9) | copy-start | bytes 18874372

commit v3 on v2

--- a/solution.py
+++ b/solution.py
@@ -466,7 +466,7 @@
     blocks = own * nmp
     nz = ndp // 2
     rows = side // ndp
-    n1 = hb // 4
+    n1 = 3 * hb // 16
 
     def inverse(table):
         hit = table[:, 0][None, :] == jnp.arange(blocks, dtype=jnp.int32)[:, None]

time: 275 us -> 272 us (0.989)
  Pallas kernels: 259 us -> 256 us
    pallas_call x1, Pallas kernels: 259 us -> 256 us  [shards_fused(): pl.pallas_call(functools.partial(fused_kernel, (ndp, nmp, hb, side, own,...]
where the time goes in v3:
time: 272 us; the launch traced here: 271 us
  Pallas kernels  256 us (94%)
  other arithmetic  9.48 us (3%)
  local copies, waits for them, and re-layouts  4.08 us (2%)
    pallas_call x1, Pallas kernels, shards_fused(): pl.pallas_call(functools.partial(fused_kernel, (ndp, nmp, hb, side, own,...  256 us

profile of v3, /device:TPU:0, one launch (start us, length us, event | category | flops | bytes accessed | tf_op | source)
XLA Modules:
  0.0 270.6 jit_solution(6360835204545627048)
XLA Ops:
  0.6 0.7 slice_bitcast_fusion.1
  1.3 0.7 slice_bitcast_fusion
  2.0 0.1 select_reduce_fusion
  2.1 0.1 fusion.2
  2.2 0.5 broadcast_select_fusion.out_inv
  2.7 0.1 select_reduce_fusion.1
  2.8 0.1 fusion.3
  2.9 0.5 broadcast_select_fusion.1.in_inv
  3.4 1.4 copy.12.in_idx
  4.8 1.4 copy.13.out_idx
  6.1 256.4 %shard_map.93 = (bf16[2,256,2048]{2,1,0:T(8,128)(2,1)}, bf16[2,256,2048]{2,1,0:T(8,128)(2,1)}, bf16[3,2,16,4,32,256]{5,4,3,2,1,0:T(8,128)(2,1)}) custom-call(s32[16,4]{1,0:T(8,128)} %copy.12.in_idx, s32[16,4]{1,0:T(8,128)} %copy.13.out_idx, s32[32]{0:T(128)} %broadcast_select_fusion.1.in_inv, s32[32]{0:T(128)} %broadcast_select_fusion.out_inv, ...), custom_call_target="tpu_custom_call" | custom-call | tf_op jit(solution)/shard_map/pallas_call | solution.py:480
  262.5 0.0 copy-start
  262.5 4.5 %fusion = (bf16[256,2048]{1,0:T(8,128)(2,1)}, bf16[256,2048]{1,0:T(8,128)(2,1)}) fusion(bf16[2,256,2048]{2,1,0:T(8,128)(2,1)} %get-tuple-element.7, bf16[2,256,2048]{2,1,0:T(8,128)(2,1)} %get-tuple-element.8), kind=kLoop, calls=%fused_computation.4 | loop fusion | flops 4194304 | bytes 6291456 | tf_op jit(solution)/shard_map/convert_element_type | solution.py:522
  267.0 0.0 copy-done
  267.0 3.5 %multiply_bitcast_fusion = (f32[16,4,32,256]{3,2,1,0:T(8,128)}, f32[16,4,32,256]{3,2,1,0:T(8,128)}) fusion(bf16[3,2,16,4,32,256]{5,4,3,2,1,0:T(8,128)(2,1)S(1)} %copy-done, pred[]{:T(512)S(6)} %lt.4, pred[]{:T(512)S(6)} %gt.4), kind=kLoop, calls=%fused_computation | loop fusion | flops 8388608 | bytes 10485762 | tf_op jit(solution)/shard_map/mul | solution.py:527
Async XLA Ops:
  262.5 4.6 %copy-start = (bf16[3,2,16,4,32,256]{5,4,3,2,1,0:T(8,128)(2,1)S(1)}, bf16[3,2,16,4,32,256]{5,4,3,2,1,0:T(8,128)(2,1)}, u32[]{:S(2)}) copy-start(bf16[3,2,16,4,32,256]{5,4,3,2,1,0:T(8,128)(2,1)} %get-tuple-element.9) | copy-start | bytes 18874372
